TPU v7x, 512 devices: a whole 4x8x8 slice. The times are simulated.
512 devices in a mesh: front: 4 (over x), row: 8 (over y), col: 16 (over z, core).
Axes of the slice: x: 4, y: 8, z: 8, core: 2. Of those that a mesh axis runs over, the one named last changes fastest.
Arguments:
- contrib: float32 [32768, 4096], P(('front', 'row'), 'col'), parts along dimension 0, as said below
- front_diag: float32 [32768], P(('front', 'row')), parts along dimension 0, may hold values from 1 to 4
- child_map: int32 [8, 32], P('front'), parts along dimension 0, may hold values from 0 to 63, as said below
- pivots: int32 [16], P('front'), parts along dimension 0, may hold values from 0 to 63, as said below
Outputs:
- lfactor: float32 [32768, 512], P(('front', 'row'), 'col'), parts along dimension 0
- schur_block: float32 [32768, 8192], P(('front', 'row'), 'col'), parts along dimension 0
There are 4 independent parts, one for each index of `front`. A program takes and returns all parts, laid end to end along the dimension named above; each array names one. Nothing has to cross between parts.
Inputs may be any that keep to these rules, and one draw needn't show every extreme that they name: child_map[c, b] is b or b + 32, chosen for each child and block. `pivots`: 4 distinct front blocks. `contrib`: each child's contribution block is symmetric positive definite.
All inputs are finite; a program needn't handle non-finite values.
Results may differ from a plain program's by a relative error of at most 0.0001.
Values sent between devices are 32-bit elements; how exact they have to be, the bound alone decides.
A program may use at most 64 MiB of HBM per device.

v0:
```python
import jax
import jax.numpy as jnp
from jax import lax
from jax.sharding import PartitionSpec as P

NF = 8192
NPAN = 2
BLK = 128
highest = lax.Precision.HIGHEST


def swapped(shard, axis, bit):
    return lax.ppermute(shard, axis, [(i, i ^ 1 << bit) for i in range(lax.axis_size(axis))])


def broadcast(shard, axis, root):
    mine = lax.axis_index(axis) == root
    return lax.psum(jnp.where(mine, shard, jnp.zeros_like(shard)), axis)


def select_rows(mapping, chosen_ids, within, half_rows, row_index, row_count, row_slots):
    by_device = mapping.reshape(mapping.shape[0] // half_rows, half_rows)
    targets = jnp.take(lax.dynamic_index_in_dim(by_device, within, 1, keepdims=False), chosen_ids)
    slot_ids = jnp.arange(row_slots) * row_count + row_index
    return (targets[None, :] == slot_ids[:, None]).astype(jnp.float32)


def select_cols(mapping, col_index, col_count, col_slots):
    by_device = mapping.reshape(mapping.shape[0] // col_count, col_count)
    targets = lax.dynamic_index_in_dim(by_device, col_index, 1, keepdims=False)
    slot_ids = jnp.arange(col_slots) * col_count + col_index
    return (targets[None, :] == slot_ids[:, None]).astype(jnp.float32)


def place_blocks(pieces, row_select, col_select):
    blocks = pieces.reshape(row_select.shape[1], BLK, col_select.shape[1], BLK)
    placed = jnp.einsum("kj,jaib->kaib", row_select, blocks, precision=highest)
    placed = jnp.einsum("li,kaib->kalb", col_select, placed, precision=highest)
    return placed.reshape(row_select.shape[0] * BLK, col_select.shape[0] * BLK)


def per_device(contrib, front_diag, child_map, pivots):
    row_count = lax.axis_size("row")
    col_count = lax.axis_size("col")
    row_index = lax.axis_index("row")
    col_index = lax.axis_index("col")
    half_rows = row_count // 2
    half_bit = half_rows.bit_length() - 1
    sibling = row_index // half_rows
    within = row_index % half_rows
    local_rows = front_diag.shape[0]
    row_slots = local_rows // BLK
    col_width = NF // col_count
    col_slots = col_width // BLK
    child_rows = contrib.shape[0] // BLK
    own_map = lax.dynamic_index_in_dim(child_map, sibling, 0, keepdims=False)
    other_map = lax.dynamic_index_in_dim(child_map, 1 - sibling, 0, keepdims=False)
    partner = swapped(contrib, "row", half_bit)
    other_ids = jnp.arange(child_rows)
    own_rows = select_rows(
        own_map, jnp.arange(child_rows), within, half_rows, row_index, row_count, row_slots
    )
    other_rows = select_rows(
        other_map, other_ids, within, half_rows, row_index, row_count, row_slots
    )
    own_cols = select_cols(own_map, col_index, col_count, col_slots)
    other_cols = select_cols(other_map, col_index, col_count, col_slots)
    assembled = place_blocks(contrib, own_rows, own_cols) + place_blocks(
        partner, other_rows, other_cols
    )
    row_ids = jnp.arange(row_slots) * row_count + row_index
    col_ids = jnp.arange(col_slots) * col_count + col_index
    on_diagonal = (row_ids[:, None] == col_ids[None, :]).astype(jnp.float32)
    identity = jnp.eye(BLK, dtype=jnp.float32)
    diag_blocks = front_diag.reshape(row_slots, BLK)
    diag_part = (
        on_diagonal[:, None, :, None] * diag_blocks[:, :, None, None] * identity[None, :, None, :]
    )
    front_tile = assembled + diag_part.reshape(local_rows, col_width)
    factors = []
    for panel_index in range(NPAN):
        chosen = [pivots[2 * panel_index], pivots[2 * panel_index + 1]]
        columns = []
        for block_id in chosen:
            block_piece = lax.dynamic_slice_in_dim(front_tile, block_id // col_count * BLK, BLK, 1)
            columns.append(broadcast(block_piece, "col", block_id % col_count))
        panel_cols = jnp.concatenate(columns, axis=1)
        owned_rows = []
        for block_id in chosen:
            rows_here = lax.dynamic_slice_in_dim(panel_cols, block_id // row_count * BLK, BLK, 0)
            owned_rows.append(jnp.where(block_id % row_count == row_index, rows_here, 0.0))
        pivot_block = lax.psum(jnp.concatenate(owned_rows, axis=0), "row")
        lower_factor = jnp.linalg.cholesky(pivot_block)
        factor = lax.linalg.triangular_solve(
            lower_factor, panel_cols, left_side=False, lower=True, transpose_a=True
        )
        source_rows = []
        for slot_index in range(col_slots):
            source_rows.append(
                lax.dynamic_slice_in_dim(factor, col_ids[slot_index] // row_count * BLK, BLK, 0)
            )
        across = broadcast(jnp.concatenate(source_rows, axis=0), "row", col_index % row_count)
        update = jnp.einsum("ak,bk->ab", factor, across, precision=highest)
        row_hit = jnp.logical_or(row_ids == chosen[0], row_ids == chosen[1])
        col_hit = jnp.logical_or(col_ids == chosen[0], col_ids == chosen[1])
        row_keep = jnp.repeat(jnp.where(row_hit, 0.0, 1.0), BLK)
        col_keep = jnp.repeat(jnp.where(col_hit, 0.0, 1.0), BLK)
        front_tile = (front_tile - update) * row_keep[:, None] * col_keep[None, :]
        factors.append(factor)
    stacked = jnp.concatenate(factors, axis=1)
    col_share = stacked.shape[1] // col_count
    lfactor = lax.dynamic_slice_in_dim(stacked, col_index * col_share, col_share, 1)
    return (lfactor, front_tile)


def solution(mesh):
    placed = (P(("front", "row"), "col"), P(("front", "row")), P("front", None), P("front"))
    return jax.shard_map(
        per_device,
        mesh=mesh,
        in_specs=placed,
        out_specs=(P(("front", "row"), "col"), P(("front", "row"), "col")),
        check_vma=False,
    )
```

profile of v0, /device:TPU:2, one launch (start us, length us, event | category | flops | bytes accessed | tf_op | source)
XLA Modules:
  0.0 781.1 jit_solution(6074221105859730015)
XLA Ops:
  7.2 7.7 collective-permute-start
  17.5 1.4 fusion.61
  19.0 1.7 reshape.126
  28.0 2.3 fusion.3
  30.4 30.0 %collective-permute-done = f32[1024,256]{1,0:T(8,128)} collective-permute-done((f32[1024,256]{1,0:T(8,128)}, f32[1024,256]{1,0:T(8,128)}, u32[]{:S(2)}, u32[]{:S(2)}) %collective-permute-start) | collective-permute-done | bytes 1048608 | tf_op jit(solution)/shard_map/ppermute | solution.py:13
  60.4 1.7 reshape.129
  63.3 3.7 bitcast_add_fusion
  67.0 1.5 copy.39
  68.5 1.9 copy.28
  71.7 123.2 %all-reduce.20.cloned.1.call-done = (f32[1024,128]{0,1:T(8,128)}, f32[1024,128]{0,1:T(8,128)}) async-done(((f32[1024,128]{0,1:T(8,128)}, f32[1024,128]{0,1:T(8,128)}), (f32[1024,128]{0,1:T(8,128)}, f32[1024,128]{0,1:T(8,128)})) %all-reduce.20.cloned.1.call-update) | async-done | bytes 1048592 | tf_op jit(solution)/shard_map/psum | solution.py:18
  215.0 60.4 %all-reduce.10.cloned.1.call-done = f32[256,256]{0,1:T(8,128)} async-done(((f32[256,256]{0,1:T(8,128)}), f32[256,256]{0,1:T(8,128)}) %all-reduce.10.cloned.1.call-update) | async-done | bytes 262160 | tf_op jit(solution)/shard_map/psum | solution.py:92
  277.5 11.7 %cholesky.130 = f32[128,128]{1,0:T(8,128)S(1)} custom-call(f32[128,128]{1,0:T(8,128)S(1)} %cholesky.194), custom_call_target="Cholesky" | custom-call | tf_op jit(solution)/shard_map/jit(cholesky)/cholesky | solution.py:93
  289.2 9.8 %custom-call.13 = f32[1,128,128]{1,2,0:T(8,128)S(1)} custom-call(f32[1,128,128]{2,1,0:T(8,128)S(1)} %get-tuple-element.74), custom_call_target="InvertDiagBlocksLowerTriangular" | custom-call | tf_op jit(solution)/shard_map/jit(cholesky)/cholesky | solution.py:93
  299.5 11.7 %cholesky.147 = f32[128,128]{1,0:T(8,128)S(1)} custom-call(f32[128,128]{1,0:T(8,128)S(1)} %convolution_subtract_fusion.3), custom_call_target="Cholesky" | custom-call | tf_op jit(solution)/shard_map/jit(cholesky)/cholesky | solution.py:93
  314.0 4.3 while.4
  314.9 1.4 bitcast_dynamic-update-slice_fusion.4
  317.0 1.4 bitcast_dynamic-update-slice_fusion.4
  318.4 19.7 %custom-call.14 = f32[2,128,128]{1,2,0:T(8,128)S(1)} custom-call(f32[2,128,128]{2,1,0:T(8,128)S(1)} %get-tuple-element.19), custom_call_target="InvertDiagBlocksLowerTriangular" | custom-call | tf_op jit(solution)/shard_map/triangular_solve/custom-call.0 | solution.py:94
  342.3 76.2 %all-reduce.12.cloned.1.call-done = f32[512,256]{0,1:T(8,128)} async-done(((f32[512,256]{0,1:T(8,128)}), f32[512,256]{0,1:T(8,128)}) %all-reduce.12.cloned.1.call-update) | async-done | bytes 524304 | tf_op jit(solution)/shard_map/psum | solution.py:18
  418.5 3.8 multiply_multiply_fusion.1
  423.5 116.7 %all-reduce.18.cloned.1.call-done = (f32[1024,128]{0,1:T(8,128)}, f32[1024,128]{0,1:T(8,128)}) async-done(((f32[1024,128]{0,1:T(8,128)}, f32[1024,128]{0,1:T(8,128)}), (f32[1024,128]{0,1:T(8,128)}, f32[1024,128]{0,1:T(8,128)})) %all-reduce.18.cloned.1.call-update) | async-done | bytes 1048592 | tf_op jit(solution)/shard_map/psum | solution.py:18
  546.0 74.6 %all-reduce.14.cloned.1.call-done = f32[256,256]{0,1:T(8,128)} async-done(((f32[256,256]{0,1:T(8,128)}), f32[256,256]{0,1:T(8,128)}) %all-reduce.14.cloned.1.call-update) | async-done | bytes 262160 | tf_op jit(solution)/shard_map/psum | solution.py:92
  622.7 11.7 %cholesky.164 = f32[128,128]{1,0:T(8,128)S(1)} custom-call(f32[128,128]{1,0:T(8,128)S(1)} %cholesky.197), custom_call_target="Cholesky" | custom-call | tf_op jit(solution)/shard_map/jit(cholesky)/cholesky | solution.py:93
  634.4 9.8 %custom-call.15 = f32[1,128,128]{1,2,0:T(8,128)S(1)} custom-call(f32[1,128,128]{2,1,0:T(8,128)S(1)} %get-tuple-element.70), custom_call_target="InvertDiagBlocksLowerTriangular" | custom-call | tf_op jit(solution)/shard_map/jit(cholesky)/cholesky | solution.py:93
  644.7 11.7 %cholesky.181 = f32[128,128]{1,0:T(8,128)S(1)} custom-call(f32[128,128]{1,0:T(8,128)S(1)} %convolution_subtract_fusion.2), custom_call_target="Cholesky" | custom-call | tf_op jit(solution)/shard_map/jit(cholesky)/cholesky | solution.py:93
  659.1 4.2 while.5
  663.3 19.7 %custom-call.16 = f32[2,128,128]{1,2,0:T(8,128)S(1)} custom-call(f32[2,128,128]{2,1,0:T(8,128)S(1)} %get-tuple-element.20), custom_call_target="InvertDiagBlocksLowerTriangular" | custom-call | tf_op jit(solution)/shard_map/triangular_solve/custom-call.0 | solution.py:94
  683.0 1.7 fusion.22
  684.7 1.7 convolution_subtract_fusion
  689.5 76.7 %all-reduce.16.cloned.1.call-done = f32[512,256]{0,1:T(8,128)} async-done(((f32[512,256]{0,1:T(8,128)}), f32[512,256]{0,1:T(8,128)}) %all-reduce.16.cloned.1.call-update) | async-done | bytes 524304 | tf_op jit(solution)/shard_map/psum | solution.py:18
  766.2 4.6 multiply_multiply_fusion
  770.8 2.9 copy.17
  (110 shorter events, 40.0 us)
Async XLA Ops:
  7.2 18.7 %copy-start.6 = (f32[1024]{0:T(1024)S(1)}, f32[1024]{0:T(1024)}, u32[]{:S(2)}) copy-start(f32[1024]{0:T(1024)} %param.10) | copy-start | bytes 12292
  7.2 187.8 %all-reduce.20.cloned.1.call-start = ((), (), s32[]{:S(2)}) async-start(), calls=%async_computation.5 | async-start | bytes 2097152 | tf_op jit(solution)/shard_map/psum | solution.py:18
  7.2 53.1 %collective-permute-start = (f32[1024,256]{1,0:T(8,128)}, f32[1024,256]{1,0:T(8,128)}, u32[]{:S(2)}, u32[]{:S(2)}) collective-permute-start(f32[1024,256]{1,0:T(8,128)} %param.9), channel_id=1, source_target_pairs={{0,64},{16,80},{32,96},{48,112},{64,0},{80,16},{96,32},{112,48},{1... | collective-permute-start | bytes 3145736 | tf_op jit(solution)/shard_map/ppermute | solution.py:13
  62.1 1.2 copy-start.5
  70.4 125.7 %copy-start = (f32[1024,512]{0,1:T(8,128)}, f32[1024,512]{0,1:T(8,128)S(1)}, u32[]{:S(2)}) copy-start(f32[1024,512]{0,1:T(8,128)S(1)} %copy.28) | copy-start | bytes 6291460
  71.6 203.7 %all-reduce.10.cloned.1.call-start = ((), (), s32[]{:S(2)}) async-start(), calls=%async_computation | async-start | bytes 524288 | tf_op jit(solution)/shard_map/psum | solution.py:92
  198.0 220.5 %all-reduce.12.cloned.1.call-start = ((), (), s32[]{:S(2)}) async-start(), calls=%async_computation.1 | async-start | bytes 1048576 | tf_op jit(solution)/shard_map/psum | solution.py:18
  208.7 129.3 %copy-start.4 = (f32[1024,128]{0,1:T(8,128)S(1)}, f32[1024,128]{0,1:T(8,128)}, u32[]{:S(2)}) copy-start(f32[1024,128]{0,1:T(8,128)} %get-tuple-element.45) | copy-start | bytes 1572868
  277.4 61.3 %copy-start.3 = (f32[1024,128]{0,1:T(8,128)S(1)}, f32[1024,128]{0,1:T(8,128)}, u32[]{:S(2)}) copy-start(f32[1024,128]{0,1:T(8,128)} %get-tuple-element.46) | copy-start | bytes 1572868
  339.9 82.4 %copy-start.1 = (f32[1024,128]{0,1:T(8,128)}, f32[1024,128]{0,1:T(8,128)S(1)}, u32[]{:S(2)}) copy-start(f32[1024,128]{0,1:T(8,128)S(1)} %fusion.25) | copy-start | bytes 1572868
  340.9 199.3 %all-reduce.18.cloned.1.call-start = ((), (), s32[]{:S(2)}) async-start(), calls=%async_computation.4 | async-start | bytes 2097152 | tf_op jit(solution)/shard_map/psum | solution.py:18
  423.4 197.2 %all-reduce.14.cloned.1.call-start = ((), (), s32[]{:S(2)}) async-start(), calls=%async_computation.2 | async-start | bytes 524288 | tf_op jit(solution)/shard_map/psum | solution.py:92
  543.2 223.1 %all-reduce.16.cloned.1.call-start = ((), (), s32[]{:S(2)}) async-start(), calls=%async_computation.3 | async-start | bytes 1048576 | tf_op jit(solution)/shard_map/psum | solution.py:18
  686.9 0.8 copy-start.2
Sparse Core Ops, SparseCore 0:
  71.7 123.1 all-reduce.19
  198.1 77.2 all-reduce.9
  341.0 77.3 all-reduce.11
  423.5 116.6 all-reduce.17
  543.3 77.2 all-reduce.13
  688.8 77.3 all-reduce.15
where the time goes:
time: 789 us; the launch traced here: 781 us
  waiting for transfers between devices  558 us (71%)
  other arithmetic  123 us (16%)
  between operations  37.4 us (5%)
  local copies, waits for them, and re-layouts  30.3 us (4%)
  matrix products  23.5 us (3%)
  starting transfers between devices  8.41 us (1%)
    psum x4, waiting for transfers between devices, broadcast(): return lax.psum(jnp.where(mine, shard, jnp.zeros_like(shard)), axis)  393 us
    psum x2, waiting for transfers between devices, per_device(): pivot_block = lax.psum(jnp.concatenate(owned_rows, axis=0), 'row')  135 us
    another operation x14, other arithmetic, per_device(): lower_factor = jnp.linalg.cholesky(pivot_block)  69.3 us
    another operation x7, other arithmetic, per_device(): lax.linalg.triangular_solve(lower_factor, panel_cols, left_side=False, lo...  39.6 us
    ppermute x1, waiting for transfers between devices, swapped(): lax.ppermute(shard, axis, [(i, i ^ 1 << bit) for i in range(lax.axis_size...  30 us
  transfers between devices with their start and end apart: 7, of which 7 were waited for; matrix products, arithmetic and copies ran while one was open for 2% of the time, Pallas kernels for 0%

commit v1 on v0

--- a/solution.py
+++ b/solution.py
@@ -89,7 +89,9 @@
         for block_id in chosen:
             rows_here = lax.dynamic_slice_in_dim(panel_cols, block_id // row_count * BLK, BLK, 0)
             owned_rows.append(jnp.where(block_id % row_count == row_index, rows_here, 0.0))
-        pivot_block = lax.psum(jnp.concatenate(owned_rows, axis=0), "row")
+        pivot_block = jnp.sum(
+            lax.all_gather(jnp.concatenate(owned_rows, axis=0), axis_name="row"), 0
+        )
         lower_factor = jnp.linalg.cholesky(pivot_block)
         factor = lax.linalg.triangular_solve(
             lower_factor, panel_cols, left_side=False, lower=True, transpose_a=True

time: 789 us -> 717 us (0.909)
  waiting for transfers between devices: 558 us -> 490 us
    psum x2 -> x0, waiting for transfers between devices: 135 us -> none  [per_device(): pivot_block = lax.psum(jnp.concatenate(owned_rows, axis=0), 'row')]
    all_gather x0 -> x2, waiting for transfers between devices: none -> 66.3 us  [per_device(): lax.all_gather(jnp.concatenate(owned_rows, axis=0), axis_name='row')]
where the time goes in v1:
time: 717 us; the launch traced here: 710 us
  waiting for transfers between devices  490 us (68%)
  other arithmetic  125 us (17%)
  between operations  38.1 us (5%)
  matrix products  24.7 us (3%)
  local copies, waits for them, and re-layouts  23.5 us (3%)
  starting transfers between devices  8.41 us (1%)
    psum x4, waiting for transfers between devices, broadcast(): return lax.psum(jnp.where(mine, shard, jnp.zeros_like(shard)), axis)  394 us
    another operation x14, other arithmetic, per_device(): lower_factor = jnp.linalg.cholesky(pivot_block)  69.3 us
    all_gather x2, waiting for transfers between devices, per_device(): lax.all_gather(jnp.concatenate(owned_rows, axis=0), axis_name='row')  66.3 us
    another operation x7, other arithmetic, per_device(): lax.linalg.triangular_solve(lower_factor, panel_cols, left_side=False, lo...  39.6 us
    ppermute x1, waiting for transfers between devices, swapped(): lax.ppermute(shard, axis, [(i, i ^ 1 << bit) for i in range(lax.axis_size...  29.6 us
  transfers between devices with their start and end apart: 7, of which 7 were waited for; matrix products, arithmetic and copies ran while one was open for 2% of the time, Pallas kernels for 0%

profile of v1, /device:TPU:2, one launch (start us, length us, event | category | flops | bytes accessed | tf_op | source)
XLA Modules:
  0.0 709.9 jit_solution(13101470090596261503)
XLA Ops:
  7.2 7.7 %collective-permute-start = (f32[1024,256]{1,0:T(8,128)}, f32[1024,256]{1,0:T(8,128)}, u32[]{:S(2)}, u32[]{:S(2)}) collective-permute-start(f32[1024,256]{1,0:T(8,128)} %param.9), channel_id=1, source_target_pairs={{0,64},{16,80},{32,96},{48,112},{64,0},{80,16},{96,32},{112,48},{1... | collective-permute-start | bytes 3145736 | tf_op jit(solution)/shard_map/ppermute | solution.py:13
  17.5 1.5 fusion.61
  19.0 1.7 reshape.126
  28.4 2.3 fusion.3
  30.8 29.6 %collective-permute-done = f32[1024,256]{1,0:T(8,128)} collective-permute-done((f32[1024,256]{1,0:T(8,128)}, f32[1024,256]{1,0:T(8,128)}, u32[]{:S(2)}, u32[]{:S(2)}) %collective-permute-start) | collective-permute-done | bytes 1048608 | tf_op jit(solution)/shard_map/ppermute | solution.py:13
  60.4 1.7 reshape.187
  63.3 3.7 bitcast_add_fusion
  69.6 123.2 %all-reduce.14.cloned.1.call-done = (f32[1024,128]{1,0:T(8,128)}, f32[1024,128]{1,0:T(8,128)}) async-done(((f32[1024,128]{1,0:T(8,128)}, f32[1024,128]{1,0:T(8,128)}), (f32[1024,128]{1,0:T(8,128)}, f32[1024,128]{1,0:T(8,128)})) %all-reduce.14.cloned.1.call-update) | async-done | bytes 1048592 | tf_op jit(solution)/shard_map/psum | solution.py:18
  213.2 25.9 %all-gather.5.cloned.1.call-done = f32[2048,256]{1,0:T(8,128)} async-done(((f32[256,256]{1,0:T(8,128)}), f32[2048,256]{1,0:T(8,128)}) %all-gather.5.cloned.1.call-update) | async-done | bytes 2097168 | tf_op jit(solution)/shard_map/all_gather | solution.py:93
  239.0 1.8 reduce_sum.18
  241.0 11.7 %cholesky.130 = f32[128,128]{1,0:T(8,128)S(1)} custom-call(f32[128,128]{1,0:T(8,128)S(1)} %cholesky.194), custom_call_target="Cholesky" | custom-call | tf_op jit(solution)/shard_map/jit(cholesky)/cholesky | solution.py:95
  252.8 9.8 %custom-call.13 = f32[1,128,128]{1,2,0:T(8,128)S(1)} custom-call(f32[1,128,128]{2,1,0:T(8,128)S(1)} %get-tuple-element.70), custom_call_target="InvertDiagBlocksLowerTriangular" | custom-call | tf_op jit(solution)/shard_map/jit(cholesky)/cholesky | solution.py:95
  263.1 11.7 %cholesky.147 = f32[128,128]{1,0:T(8,128)S(1)} custom-call(f32[128,128]{1,0:T(8,128)S(1)} %convolution_subtract_fusion.3), custom_call_target="Cholesky" | custom-call | tf_op jit(solution)/shard_map/jit(cholesky)/cholesky | solution.py:95
  277.5 4.1 while.4
  278.4 1.3 bitcast_dynamic-update-slice_fusion.4
  281.6 19.7 %custom-call.14 = f32[2,128,128]{1,2,0:T(8,128)S(1)} custom-call(f32[2,128,128]{2,1,0:T(8,128)S(1)} %get-tuple-element.19), custom_call_target="InvertDiagBlocksLowerTriangular" | custom-call | tf_op jit(solution)/shard_map/triangular_solve/custom-call.0 | solution.py:96
  306.1 76.5 %all-reduce.8.cloned.1.call-done = f32[512,256]{0,1:T(8,128)} async-done(((f32[512,256]{0,1:T(8,128)}), f32[512,256]{0,1:T(8,128)}) %all-reduce.8.cloned.1.call-update) | async-done | bytes 524304 | tf_op jit(solution)/shard_map/psum | solution.py:18
  382.6 4.0 multiply_multiply_fusion.1
  387.9 116.9 %all-reduce.12.cloned.1.call-done = (f32[1024,128]{1,0:T(8,128)}, f32[1024,128]{1,0:T(8,128)}) async-done(((f32[1024,128]{1,0:T(8,128)}, f32[1024,128]{1,0:T(8,128)}), (f32[1024,128]{1,0:T(8,128)}, f32[1024,128]{1,0:T(8,128)})) %all-reduce.12.cloned.1.call-update) | async-done | bytes 1048592 | tf_op jit(solution)/shard_map/psum | solution.py:18
  510.6 40.4 %all-gather.7.cloned.1.call-done = f32[2048,256]{1,0:T(8,128)} async-done(((f32[256,256]{1,0:T(8,128)}), f32[2048,256]{1,0:T(8,128)}) %all-gather.7.cloned.1.call-update) | async-done | bytes 2097168 | tf_op jit(solution)/shard_map/all_gather | solution.py:93
  551.0 1.8 reduce_sum.19
  553.0 11.7 %cholesky.164 = f32[128,128]{1,0:T(8,128)S(1)} custom-call(f32[128,128]{1,0:T(8,128)S(1)} %cholesky.197), custom_call_target="Cholesky" | custom-call | tf_op jit(solution)/shard_map/jit(cholesky)/cholesky | solution.py:95
  564.7 9.8 %custom-call.15 = f32[1,128,128]{1,2,0:T(8,128)S(1)} custom-call(f32[1,128,128]{2,1,0:T(8,128)S(1)} %get-tuple-element.66), custom_call_target="InvertDiagBlocksLowerTriangular" | custom-call | tf_op jit(solution)/shard_map/jit(cholesky)/cholesky | solution.py:95
  575.0 11.7 %cholesky.181 = f32[128,128]{1,0:T(8,128)S(1)} custom-call(f32[128,128]{1,0:T(8,128)S(1)} %convolution_subtract_fusion.2), custom_call_target="Cholesky" | custom-call | tf_op jit(solution)/shard_map/jit(cholesky)/cholesky | solution.py:95
  589.5 4.4 while.5
  590.4 1.4 bitcast_dynamic-update-slice_fusion.5
  592.5 1.4 bitcast_dynamic-update-slice_fusion.5
  593.9 19.7 %custom-call.16 = f32[2,128,128]{1,2,0:T(8,128)S(1)} custom-call(f32[2,128,128]{2,1,0:T(8,128)S(1)} %get-tuple-element.20), custom_call_target="InvertDiagBlocksLowerTriangular" | custom-call | tf_op jit(solution)/shard_map/triangular_solve/custom-call.0 | solution.py:96
  613.6 1.7 fusion.22
  615.3 2.0 convolution_subtract_fusion
  620.6 77.2 %all-reduce.10.cloned.1.call-done = f32[512,256]{0,1:T(8,128)} async-done(((f32[512,256]{0,1:T(8,128)}), f32[512,256]{0,1:T(8,128)}) %all-reduce.10.cloned.1.call-update) | async-done | bytes 524304 | tf_op jit(solution)/shard_map/psum | solution.py:18
  697.8 4.8 multiply_multiply_fusion
  (110 shorter events, 36.7 us)
Async XLA Ops:
  7.2 19.1 %copy-start.6 = (f32[1024]{0:T(1024)S(1)}, f32[1024]{0:T(1024)}, u32[]{:S(2)}) copy-start(f32[1024]{0:T(1024)} %param.10) | copy-start | bytes 12292
  7.2 185.6 %all-reduce.14.cloned.1.call-start = ((), (), s32[]{:S(2)}) async-start(), calls=%async_computation.5 | async-start | bytes 2097152 | tf_op jit(solution)/shard_map/psum | solution.py:18
  7.2 53.1 %collective-permute-start = (f32[1024,256]{1,0:T(8,128)}, f32[1024,256]{1,0:T(8,128)}, u32[]{:S(2)}, u32[]{:S(2)}) collective-permute-start(f32[1024,256]{1,0:T(8,128)} %param.9), channel_id=1, source_target_pairs={{0,64},{16,80},{32,96},{48,112},{64,0},{80,16},{96,32},{112,48},{1... | collective-permute-start | bytes 3145736 | tf_op jit(solution)/shard_map/ppermute | solution.py:13
  62.1 1.2 copy-start.5
  67.0 1.3 copy-start
  69.5 169.6 %all-gather.5.cloned.1.call-start = ((), (), s32[]{:S(2)}) async-start(), calls=%async_computation.2 | async-start | bytes 2359296 | tf_op jit(solution)/shard_map/all_gather | solution.py:93
  195.8 186.8 %all-reduce.8.cloned.1.call-start = ((), (), s32[]{:S(2)}) async-start(), calls=%async_computation | async-start | bytes 1048576 | tf_op jit(solution)/shard_map/psum | solution.py:18
  240.8 60.5 %copy-start.4 = (f32[1024,128]{1,0:T(8,128)S(1)}, f32[1024,128]{1,0:T(8,128)}, u32[]{:S(2)}) copy-start(f32[1024,128]{1,0:T(8,128)} %get-tuple-element.41) | copy-start | bytes 1572868
  241.0 61.0 %copy-start.3 = (f32[1024,128]{1,0:T(8,128)S(1)}, f32[1024,128]{1,0:T(8,128)}, u32[]{:S(2)}) copy-start(f32[1024,128]{1,0:T(8,128)} %get-tuple-element.42) | copy-start | bytes 1572868
  303.6 83.0 %copy-start.1 = (f32[1024,128]{0,1:T(8,128)}, f32[1024,128]{0,1:T(8,128)S(1)}, u32[]{:S(2)}) copy-start(f32[1024,128]{0,1:T(8,128)S(1)} %fusion.25) | copy-start | bytes 1572868
  304.6 200.2 %all-reduce.12.cloned.1.call-start = ((), (), s32[]{:S(2)}) async-start(), calls=%async_computation.4 | async-start | bytes 2097152 | tf_op jit(solution)/shard_map/psum | solution.py:18
  387.8 163.2 %all-gather.7.cloned.1.call-start = ((), (), s32[]{:S(2)}) async-start(), calls=%async_computation.3 | async-start | bytes 2359296 | tf_op jit(solution)/shard_map/all_gather | solution.py:93
  507.8 190.0 %all-reduce.10.cloned.1.call-start = ((), (), s32[]{:S(2)}) async-start(), calls=%async_computation.1 | async-start | bytes 1048576 | tf_op jit(solution)/shard_map/psum | solution.py:18
  618.0 0.8 copy-start.2
Sparse Core Ops, SparseCore 0:
  69.6 123.1 all-reduce.13
  195.9 43.0 all-gather.4
  304.7 77.8 all-reduce.7
  387.9 116.8 all-reduce.11
  507.9 43.0 all-gather.6
  619.9 77.8 all-reduce.9
